TPU v7x, 512 devices: a whole 4x8x8 slice. The times are simulated.
512 devices in a mesh: dp: 2 (over y_hi), gx: 32 (over x, z), gy: 8 (over y_lo, core).
Axes of the slice: x: 4, y: 8 (y_hi: 2, y_lo: 4; y = y_hi * 4 + y_lo), z: 8, core: 2. Of those that a mesh axis runs over, the one named last changes fastest.
Arguments:
- fields: bfloat16 [2, 16, 256, 32768], P('dp', None, 'gx', 'gy'), may hold values from -6 to 6
- pre_act: bfloat16 [2, 16, 256, 32768], P('dp', None, 'gx', 'gy'), may hold values from -6 to 6
- cotangent: bfloat16 [2, 16, 256, 32768], P('dp', None, 'gx', 'gy'), may hold values from -6 to 6
- spec_weight: bfloat16 [2, 32, 32, 16, 256], P(None, 'gx', None, 'gy'), may hold values from -12 to 12
- point_weight: bfloat16 [16, 16], replicated, may hold values from -1.5 to 1.5
Outputs:
- grad_fields: bfloat16 [2, 16, 256, 32768], P('dp', None, 'gx', 'gy')
- grad_spec: float32 [2, 32, 32, 16, 256], P(None, 'gx', None, 'gy')
All inputs are finite; a program needn't handle non-finite values.
Results may differ from a plain program's by a relative error of at most 0.0098.
Values may be sent and summed in bfloat16 or wider, within the bound.
No kernel may reach another device: no remote copies, remote signals or barrier semaphores. Data moves between devices by JAX's collectives and lax.ppermute only.
A program may use at most 64 MiB of HBM per device.

v0:
```python
import math
import jax
import jax.numpy as jnp
from jax import lax
from jax.sharding import PartitionSpec as P

C = 16
NX = 256
NY = 512
NZ = 64
MX = 32
MY = 32
MZ = 16


def kept_freqs(kept, length, both_signs):
    index = jnp.arange(kept, dtype=jnp.int32)
    if both_signs:
        return jnp.where(index < kept // 2, index, length - kept + index)
    return index


def phase(freqs, points, length):
    turns = points[:, None] * freqs[None, :] % length
    return turns.astype(jnp.float32) * (2.0 * math.pi / length)


def forward_table(kept, length):
    angle = phase(kept_freqs(kept, length, True), jnp.arange(length, dtype=jnp.int32), length)
    cosine = jnp.cos(angle)
    minus_sine = -jnp.sin(angle)
    upper = jnp.stack([cosine, minus_sine], axis=-1)
    lower = jnp.stack([-minus_sine, cosine], axis=-1)
    return jnp.stack([upper, lower], axis=1).astype(jnp.bfloat16)


def inverse_table(kept, length, positions):
    angle = phase(kept_freqs(kept, length, True), positions, length)
    cosine = jnp.transpose(jnp.cos(angle))
    sine = jnp.transpose(jnp.sin(angle))
    upper = jnp.stack([cosine, sine], axis=-1)
    lower = jnp.stack([-sine, cosine], axis=-1)
    return jnp.stack([upper, lower], axis=1).astype(jnp.bfloat16)


def z_forward_table():
    angle = phase(kept_freqs(MZ, NZ, False), jnp.arange(NZ, dtype=jnp.int32), NZ)
    return (
        jnp.stack([jnp.cos(angle), -jnp.sin(angle)], axis=-1)
        .reshape(NZ, 2 * MZ)
        .astype(jnp.bfloat16)
    )


def z_inverse_table():
    angle = jnp.transpose(phase(kept_freqs(MZ, NZ, False), jnp.arange(NZ, dtype=jnp.int32), NZ))
    return (
        jnp.stack([jnp.cos(angle), -jnp.sin(angle)], axis=1)
        .reshape(2 * MZ, NZ)
        .astype(jnp.bfloat16)
    )


def gelu_slope(value):
    cdf = 0.5 * (1.0 + jax.scipy.special.erf(value * (1.0 / math.sqrt(2.0))))
    return cdf + value * jnp.exp(-0.5 * value * value) * (1.0 / math.sqrt(2.0 * math.pi))


def scale_modes(mode_values, weight_z):
    return mode_values.astype(jnp.float32) * weight_z[:, None]


def weight_grads(field_hat, grad_scaled):
    highest = lax.Precision.HIGHEST
    real_u = field_hat[..., 0].astype(jnp.float32)
    imag_u = field_hat[..., 1].astype(jnp.float32)
    real_d = grad_scaled[..., 0]
    imag_d = grad_scaled[..., 1]
    form = "bixyz,boxyz->xyzio"
    real_w = jnp.einsum(form, real_u, real_d, precision=highest) + jnp.einsum(
        form, imag_u, imag_d, precision=highest
    )
    imag_w = jnp.einsum(form, real_u, imag_d, precision=highest) - jnp.einsum(
        form, imag_u, real_d, precision=highest
    )
    result = jnp.stack([real_w, imag_w], axis=0)
    return result.reshape(result.shape[:4] + (C * C,))


def input_grads(spec_weight, grad_scaled):
    highest = lax.Precision.HIGHEST
    weights = spec_weight.astype(jnp.float32).reshape(spec_weight.shape[:4] + (C, C))
    real_d = grad_scaled[..., 0]
    imag_d = grad_scaled[..., 1]
    form = "xyzio,boxyz->bixyz"
    real_g = jnp.einsum(form, weights[0], real_d, precision=highest) + jnp.einsum(
        form, weights[1], imag_d, precision=highest
    )
    imag_g = jnp.einsum(form, weights[0], imag_d, precision=highest) - jnp.einsum(
        form, weights[1], real_d, precision=highest
    )
    return jnp.stack([real_g, imag_g], axis=-1).astype(jnp.bfloat16)


def on_device(fields, pre_act, cotangent, spec_weight, point_weight):
    count_x = lax.axis_size("gx")
    count_y = lax.axis_size("gy")
    local_batch, channels, local_x, local_yz = fields.shape
    local_y = local_yz // NZ
    sub_y = local_y // count_x
    local_mx = spec_weight.shape[1]
    local_mz = spec_weight.shape[3]
    stack_rows = 2 * local_batch * channels
    half_rows = local_batch * channels
    grad_pre = (cotangent.astype(jnp.float32) * gelu_slope(pre_act.astype(jnp.float32))).astype(
        jnp.bfloat16
    )
    stacked = jnp.concatenate([fields, grad_pre], axis=0)
    z_forward = z_forward_table()
    arrived = lax.all_to_all(
        stacked.reshape(stack_rows, local_x, local_yz),
        "gx",
        split_axis=2,
        concat_axis=1,
        tiled=True,
    )
    z_spectra = jnp.dot(
        arrived.reshape(stack_rows, NX, sub_y, NZ), z_forward, preferred_element_type=jnp.float32
    ).astype(jnp.bfloat16)
    z_spectra = z_spectra.reshape(stack_rows, NX, sub_y, MZ, 2)
    x_spectra = jnp.einsum(
        "sxyzr,xrkq->skyzq", z_spectra, forward_table(MX, NX), preferred_element_type=jnp.float32
    ).astype(jnp.bfloat16)
    x_spectra = x_spectra.reshape(stack_rows, MX, sub_y, 2 * MZ)
    mode_lines = lax.all_to_all(
        lax.all_to_all(x_spectra, "gx", split_axis=1, concat_axis=2, tiled=True),
        "gy",
        split_axis=3,
        concat_axis=2,
        tiled=True,
    )
    mode_lines = mode_lines.reshape(stack_rows, local_mx, NY, local_mz, 2)
    spectrum = jnp.einsum(
        "skyzr,yrlq->sklzq", mode_lines, forward_table(MY, NY), preferred_element_type=jnp.float32
    ).astype(jnp.bfloat16)
    spectrum = spectrum.reshape(2, local_batch, channels, local_mx, MY, local_mz, 2)
    field_hat = spectrum[0]
    grad_hat_in = spectrum[1]
    kz_index = lax.axis_index("gy") * local_mz + jnp.arange(local_mz, dtype=jnp.int32)
    weight_z = jnp.where(kz_index == 0, 1.0, 2.0).astype(jnp.float32) / float(NX * NY * NZ)
    grad_scaled = scale_modes(grad_hat_in, weight_z)
    grad_spec = lax.psum(weight_grads(field_hat, grad_scaled).astype(jnp.bfloat16), "dp").astype(
        jnp.float32
    )
    grad_hat = input_grads(spec_weight, grad_scaled).reshape(half_rows, local_mx, MY, local_mz, 2)
    span = count_y * sub_y
    order = jnp.arange(NY, dtype=jnp.int32)
    block = order // span
    rest = order % span
    positions = rest // sub_y * local_y + block * sub_y + rest % sub_y
    back_y = jnp.einsum(
        "sklzr,lryq->skyzq",
        grad_hat,
        inverse_table(MY, NY, positions),
        preferred_element_type=jnp.float32,
    ).astype(jnp.bfloat16)
    back_y = back_y.reshape(half_rows, local_mx, NY, 2 * local_mz)
    spread = lax.all_to_all(
        lax.all_to_all(back_y, "gx", split_axis=2, concat_axis=1, tiled=True),
        "gy",
        split_axis=2,
        concat_axis=3,
        tiled=True,
    )
    spread = spread.reshape(half_rows, MX, sub_y, MZ, 2)
    back_x = jnp.einsum(
        "skyzr,krxq->sxyzq",
        spread,
        inverse_table(MX, NX, jnp.arange(NX, dtype=jnp.int32)),
        preferred_element_type=jnp.float32,
    ).astype(jnp.bfloat16)
    returned = lax.all_to_all(
        back_x.reshape(half_rows, NX, sub_y * 2 * MZ), "gx", split_axis=1, concat_axis=2, tiled=True
    )
    spectral = jnp.dot(
        returned.reshape(half_rows, local_x, local_y, 2 * MZ),
        z_inverse_table(),
        preferred_element_type=jnp.float32,
    )
    spectral = spectral.reshape(local_batch, channels, local_x, local_yz)
    pointwise = jnp.einsum(
        "io,boxq->bixq", point_weight, grad_pre, preferred_element_type=jnp.float32
    )
    grad_fields = (spectral + pointwise).astype(jnp.bfloat16)
    return (grad_fields, grad_spec)


def solution(mesh):
    placed = (
        P("dp", None, "gx", "gy"),
        P("dp", None, "gx", "gy"),
        P("dp", None, "gx", "gy"),
        P(None, "gx", None, "gy", None),
        P(),
    )
    return jax.shard_map(
        on_device,
        mesh=mesh,
        in_specs=placed,
        out_specs=(P("dp", None, "gx", "gy"), P(None, "gx", None, "gy", None)),
        check_vma=False,
    )
```

profile of v0, /device:TPU:1, one launch (start us, length us, event | category | flops | bytes accessed | tf_op | source)
XLA Modules:
  0.0 255.6 jit_solution(6188466090925207576)
XLA Ops:
  7.2 2.3 fusion.11
  9.7 8.1 %copy.200 = bf16[32,8,4096]{0,1,2:T(8,128)(2,1)} copy(bf16[32,8,4096]{2,1,0:T(8,128)(2,1)S(1)} %bitcast.226) | data formatting | bytes 4194304 | tf_op jit(solution)/shard_map/reshape | solution.py:121
  17.8 13.3 %reshape.1022 = bf16[32,2,16384]{2,1,0:T(2,128)(2,1)} reshape(bf16[4096,8,32]{2,1,0:T(8,128)(2,1)} %bitcast.223) | data formatting | bytes 4194304
  31.1 13.8 %all-to-all-start = ((bf16[32,2,16384]{2,1,0:T(2,128)(2,1)}), bf16[32,2,16384]{2,1,0:T(2,128)(2,1)S(1)}, u32[]{:S(2)}, u32[]{:S(2)}) async-start(bf16[32,2,16384]{2,1,0:T(2,128)(2,1)} %reshape.1022), calls=%async_computation | async-start | bytes 4194304 | tf_op jit(solution)/shard_map/all_to_all | solution.py:120
  45.7 48.1 %all-to-all-done = bf16[32,2,16384]{2,1,0:T(2,128)(2,1)S(1)} async-done(((bf16[32,2,16384]{2,1,0:T(2,128)(2,1)}), bf16[32,2,16384]{2,1,0:T(2,128)(2,1)S(1)}, u32[]{:S(2)}, u32[]{:S(2)}) %all-to-all-start) | async-done | bytes 2097184 | tf_op jit(solution)/shard_map/all_to_all | solution.py:120
  93.9 6.6 %reshape.1023 = bf16[4096,8,32]{2,1,0:T(8,128)(2,1)} reshape(bf16[32,2,16384]{2,1,0:T(2,128)(2,1)S(1)} %all-to-all-done) | data formatting | bytes 4194304
  100.4 9.2 %copy.202 = bf16[32,32,8,128]{3,2,1,0:T(8,128)(2,1)S(1)} copy(bf16[32,32,8,128]{0,2,3,1:T(8,128)(2,1)} %bitcast.224) | data formatting | bytes 4194304 | tf_op jit(solution)/shard_map/all_to_all | solution.py:120
  109.7 3.3 %reshape.979 = bf16[32,256,2,64]{3,2,1,0:T(2,128)(2,1)} reshape(bf16[32,32,8,128]{3,2,1,0:T(8,128)(2,1)S(1)} %copy.202) | data formatting | bytes 4194304 | tf_op jit(solution)/shard_map/reshape | solution.py:128
  113.0 3.7 %fusion.12 = bf16[32,256,2,32]{1,3,2,0:T(8,128)(2,1)S(1)} fusion(bf16[64,32,1,1]{0,1,3,2:T(8,128)(2,1)S(1)} %bitcast.246, bf16[32,256,2,64]{3,2,1,0:T(2,128)(2,1)} %reshape.979), kind=kOutput, calls=%fused_computation.18 | convolution fusion | flops 67633152 | bytes 3149824 | tf_op jit(solution)/shard_map/dot_general | solution.py:127
  120.6 7.0 %all-to-all-start.1 = ((bf16[32,2,1024]{2,1,0:T(2,128)(2,1)}), bf16[32,2,1024]{2,1,0:T(2,128)(2,1)S(1)}, u32[]{:S(2)}, u32[]{:S(2)}) async-start(bf16[32,2,1024]{2,1,0:T(2,128)(2,1)} %reshape.1024), calls=%async_computation.1 | async-start | bytes 262144 | tf_op jit(solution)/shard_map/all_to_all | solution.py:136
  128.3 8.5 %all-to-all-done.1 = bf16[32,2,1024]{2,1,0:T(2,128)(2,1)S(1)} async-done(((bf16[32,2,1024]{2,1,0:T(2,128)(2,1)}), bf16[32,2,1024]{2,1,0:T(2,128)(2,1)S(1)}, u32[]{:S(2)}, u32[]{:S(2)}) %all-to-all-start.1) | async-done | bytes 131104 | tf_op jit(solution)/shard_map/all_to_all | solution.py:136
  138.5 7.2 %all-to-all-start.2 = ((bf16[8,2,4096]{2,1,0:T(2,128)(2,1)}), bf16[8,2,4096]{2,1,0:T(2,128)(2,1)S(1)}, u32[]{:S(2)}, u32[]{:S(2)}) async-start(bf16[8,2,4096]{2,1,0:T(2,128)(2,1)} %reshape.1026), calls=%async_computation.2 | async-start | bytes 262144 | tf_op jit(solution)/shard_map/all_to_all | solution.py:135
  145.8 5.7 %all-to-all-done.2 = bf16[8,2,4096]{2,1,0:T(2,128)(2,1)S(1)} async-done(((bf16[8,2,4096]{2,1,0:T(2,128)(2,1)}), bf16[8,2,4096]{2,1,0:T(2,128)(2,1)S(1)}, u32[]{:S(2)}, u32[]{:S(2)}) %all-to-all-start.2) | async-done | bytes 131104 | tf_op jit(solution)/shard_map/all_to_all | solution.py:135
  153.9 12.2 %all_to_all.84 = bf16[32,2,512]{2,1,0:T(2,128)(2,1)S(1)} all-to-all(bf16[32,2,512]{2,1,0:T(2,128)(2,1)S(1)} %reshape.1028), channel_id=1, replica_groups=mesh['dp'=2,'gx'=32,'gy'=8] {'gx'}, dimensions={0} | all-to-all | bytes 131072 | tf_op jit(solution)/shard_map/all_to_all | solution.py:169
  167.9 5.7 %all-to-all-start.4 = ((bf16[8,2,2048]{2,1,0:T(2,128)(2,1)}), bf16[8,2,2048]{2,1,0:T(2,128)(2,1)S(1)}, u32[]{:S(2)}, u32[]{:S(2)}) async-start(bf16[8,2,2048]{2,1,0:T(2,128)(2,1)} %reshape.1030), calls=%async_computation.4 | async-start | bytes 131072 | tf_op jit(solution)/shard_map/all_to_all | solution.py:168
  173.8 4.9 %all-to-all-done.4 = bf16[8,2,2048]{2,1,0:T(2,128)(2,1)S(1)} async-done(((bf16[8,2,2048]{2,1,0:T(2,128)(2,1)}), bf16[8,2,2048]{2,1,0:T(2,128)(2,1)S(1)}, u32[]{:S(2)}, u32[]{:S(2)}) %all-to-all-start.4) | async-done | bytes 65568 | tf_op jit(solution)/shard_map/all_to_all | solution.py:168
  182.4 3.9 %all-to-all-start.5 = ((bf16[32,2,4096]{2,1,0:T(2,128)(2,1)}), bf16[32,2,4096]{2,1,0:T(2,128)(2,1)S(1)}, u32[]{:S(2)}, u32[]{:S(2)}) async-start(bf16[32,2,4096]{2,1,0:T(2,128)(2,1)} %reshape.1032), calls=%async_computation.5 | async-start | bytes 1048576 | tf_op jit(solution)/shard_map/all_to_all | solution.py:182
  187.6 44.5 %all-reduce.2.cloned.1.call-done = bf16[2,1,32,2,256]{4,2,3,1,0:T(8,128)(2,1)} async-done(((bf16[2,1,32,2,256]{4,2,3,1,0:T(8,128)(2,1)}), bf16[2,1,32,2,256]{4,2,3,1,0:T(8,128)(2,1)}) %all-reduce.2.cloned.1.call-update) | async-done | bytes 65552 | tf_op jit(solution)/shard_map/psum | solution.py:152
  232.1 1.6 copy.230
  234.4 1.7 copy.222
  236.0 2.7 %reshape.990 = bf16[16,8,64,32]{3,2,1,0:T(8,128)(2,1)S(1)} reshape(bf16[16,8,32,64]{3,2,1,0:T(8,128)(2,1)} %copy.222) | data formatting | bytes 1048576 | tf_op jit(solution)/shard_map/reshape | solution.py:186
  238.7 2.6 %fusion.103 = f32[16,8,64,64]{3,2,1,0:T(8,128)} fusion(bf16[16,8,64,32]{3,2,1,0:T(8,128)(2,1)S(1)} %reshape.990, bf16[32,64,1,1]{1,0,3,2:T(8,128)(2,1)S(1)} %bitcast.247), kind=kOutput, calls=%fused_computation.190 | convolution fusion | flops 33554432 | bytes 2625536 | tf_op jit(solution)/shard_map/dot_general | solution.py:185
  241.4 3.5 %reshape.991 = f32[1,16,8,4096]{3,2,1,0:T(8,128)S(1)} reshape(f32[16,8,64,64]{3,2,1,0:T(8,128)} %fusion.103) | data formatting | bytes 4194304 | tf_op jit(solution)/shard_map/reshape | solution.py:190
  244.9 2.3 fusion.1
  (69 shorter events, 18.8 us)
Async XLA Ops:
  7.2 237.8 %copy-start = (bf16[16,16]{1,0:T(8,128)(2,1)S(1)}, bf16[16,16]{1,0:T(8,128)(2,1)}, u32[]{:S(2)}) copy-start(bf16[16,16]{1,0:T(8,128)(2,1)} %param.9) | copy-start | bytes 1540
  7.2 2.3 copy-start.1
  31.1 14.2 %copy-start.2 = (bf16[2,1,32,2,256]{4,3,2,1,0:T(2,128)(2,1)S(1)}, bf16[2,1,32,2,256]{4,3,2,1,0:T(2,128)(2,1)}, u32[]{:S(2)}) copy-start(bf16[2,1,32,2,256]{4,3,2,1,0:T(2,128)(2,1)} %param.8) | copy-start | bytes 196612
  31.1 62.7 %all-to-all-start = ((bf16[32,2,16384]{2,1,0:T(2,128)(2,1)}), bf16[32,2,16384]{2,1,0:T(2,128)(2,1)S(1)}, u32[]{:S(2)}, u32[]{:S(2)}) async-start(bf16[32,2,16384]{2,1,0:T(2,128)(2,1)} %reshape.1022), calls=%async_computation | async-start | bytes 4194304 | tf_op jit(solution)/shard_map/all_to_all | solution.py:120
  120.6 16.2 %all-to-all-start.1 = ((bf16[32,2,1024]{2,1,0:T(2,128)(2,1)}), bf16[32,2,1024]{2,1,0:T(2,128)(2,1)S(1)}, u32[]{:S(2)}, u32[]{:S(2)}) async-start(bf16[32,2,1024]{2,1,0:T(2,128)(2,1)} %reshape.1024), calls=%async_computation.1 | async-start | bytes 262144 | tf_op jit(solution)/shard_map/all_to_all | solution.py:136
  138.5 13.0 %all-to-all-start.2 = ((bf16[8,2,4096]{2,1,0:T(2,128)(2,1)}), bf16[8,2,4096]{2,1,0:T(2,128)(2,1)S(1)}, u32[]{:S(2)}, u32[]{:S(2)}) async-start(bf16[8,2,4096]{2,1,0:T(2,128)(2,1)} %reshape.1026), calls=%async_computation.2 | async-start | bytes 262144 | tf_op jit(solution)/shard_map/all_to_all | solution.py:135
  167.9 10.7 %all-to-all-start.4 = ((bf16[8,2,2048]{2,1,0:T(2,128)(2,1)}), bf16[8,2,2048]{2,1,0:T(2,128)(2,1)S(1)}, u32[]{:S(2)}, u32[]{:S(2)}) async-start(bf16[8,2,2048]{2,1,0:T(2,128)(2,1)} %reshape.1030), calls=%async_computation.4 | async-start | bytes 131072 | tf_op jit(solution)/shard_map/all_to_all | solution.py:168
  182.4 51.3 %all-to-all-start.5 = ((bf16[32,2,4096]{2,1,0:T(2,128)(2,1)}), bf16[32,2,4096]{2,1,0:T(2,128)(2,1)S(1)}, u32[]{:S(2)}, u32[]{:S(2)}) async-start(bf16[32,2,4096]{2,1,0:T(2,128)(2,1)} %reshape.1032), calls=%async_computation.5 | async-start | bytes 1048576 | tf_op jit(solution)/shard_map/all_to_all | solution.py:182
  186.3 45.8 %all-reduce.2.cloned.1.call-start = ((), (), s32[]{:S(2)}) async-start(), calls=%async_computation.6 | async-start | bytes 131072 | tf_op jit(solution)/shard_map/psum | solution.py:152
Sparse Core Ops, SparseCore 0:
  190.5 41.5 all-reduce.1
where the time goes:
time: 257 us; the launch traced here: 256 us
  waiting for transfers between devices  112 us (44%)
  local copies, waits for them, and re-layouts  64.1 us (25%)
  starting transfers between devices  37.9 us (15%)
  between operations  14.5 us (6%)
  blocking collectives  12.2 us (5%)
  matrix products  10.3 us (4%)
  other arithmetic  4.89 us (2%)
    all_to_all x1, waiting for transfers between devices, on_device(): lax.all_to_all(stacked.reshape(stack_rows, local_x, local_yz), 'gx', spli...  48.1 us
    psum x1, waiting for transfers between devices, on_device(): lax.psum(weight_grads(field_hat, grad_scaled).astype(jnp.bfloat16), 'dp')  44.5 us
    unnamed x23, local copies, waits for them, and re-layouts  30.1 us
    all_to_all x1, starting transfers between devices, on_device(): lax.all_to_all(stacked.reshape(stack_rows, local_x, local_yz), 'gx', spli...  13.8 us
    all_to_all x1, blocking collectives, on_device(): lax.all_to_all(back_y, 'gx', split_axis=2, concat_axis=1, tiled=True)  12.2 us
    all_to_all x1, local copies, waits for them, and re-layouts, on_device(): lax.all_to_all(stacked.reshape(stack_rows, local_x, local_yz), 'gx', spli...  9.24 us
    all_to_all x1, waiting for transfers between devices, on_device(): lax.all_to_all(x_spectra, 'gx', split_axis=1, concat_axis=2, tiled=True)  8.52 us
    reshape x1, local copies, waits for them, and re-layouts, on_device(): stacked.reshape(stack_rows, local_x, local_yz)  8.08 us
  transfers between devices with their start and end apart: 6, of which 5 were waited for; matrix products, arithmetic and copies ran while one was open for 2% of the time, Pallas kernels for 0%

commit v1 on v0

--- a/solution.py
+++ b/solution.py
@@ -3,6 +3,7 @@
 import jax.numpy as jnp
 from jax import lax
 from jax.sharding import PartitionSpec as P
+from jax.lax import all_gather
 
 C = 16
 NX = 256
@@ -149,9 +150,9 @@
     kz_index = lax.axis_index("gy") * local_mz + jnp.arange(local_mz, dtype=jnp.int32)
     weight_z = jnp.where(kz_index == 0, 1.0, 2.0).astype(jnp.float32) / float(NX * NY * NZ)
     grad_scaled = scale_modes(grad_hat_in, weight_z)
-    grad_spec = lax.psum(weight_grads(field_hat, grad_scaled).astype(jnp.bfloat16), "dp").astype(
-        jnp.float32
-    )
+    grad_spec = jnp.sum(
+        all_gather(weight_grads(field_hat, grad_scaled).astype(jnp.bfloat16), axis_name="dp"), 0
+    ).astype(jnp.float32)
     grad_hat = input_grads(spec_weight, grad_scaled).reshape(half_rows, local_mx, MY, local_mz, 2)
     span = count_y * sub_y
     order = jnp.arange(NY, dtype=jnp.int32)

time: 257 us -> 213 us (0.83)
  waiting for transfers between devices: 112 us -> 80.9 us
  between operations: 14.5 us -> 1.08 us
  blocking collectives: 12.2 us -> 8.01 us
  starting transfers between devices: 37.9 us -> 41.2 us
    psum x1 -> x0, waiting for transfers between devices: 44.5 us -> none  [on_device(): lax.psum(weight_grads(field_hat, grad_scaled).astype(jnp.bfloat16), 'dp')]
    all_to_all x1 -> x0, blocking collectives: 12.2 us -> none  [on_device(): lax.all_to_all(back_y, 'gx', split_axis=2, concat_axis=1, tiled=True)]
    all_to_all x0 -> x1, waiting for transfers between devices: none -> 8.58 us  [on_device(): lax.all_to_all(back_y, 'gx', split_axis=2, concat_axis=1, tiled=True)]
    all_gather x0 -> x1, blocking collectives: none -> 8.01 us  [on_device(): all_gather(weight_grads(field_hat, grad_scaled).astype(jnp.bfloat16), axi...]
    all_to_all x1, waiting for transfers between devices: 0.01 us -> 4.85 us  [on_device(): lax.all_to_all(back_x.reshape(half_rows, NX, sub_y * 2 * MZ), 'gx', split...]
    all_to_all x0 -> x1, starting transfers between devices: none -> 3.85 us  [on_device(): lax.all_to_all(back_y, 'gx', split_axis=2, concat_axis=1, tiled=True)]
    unnamed x23 -> x24, local copies, waits for them, and re-layouts: 30.1 us -> 30.1 us
  transfers between devices with their start and end apart: 6 -> 6, of which waited for: 5 -> 6; matrix products, arithmetic and copies ran while one was open for 2% -> 1% of each run, Pallas kernels for 0% -> 0%
where the time goes in v1:
time: 213 us; the launch traced here: 210 us
  waiting for transfers between devices  80.9 us (38%)
  local copies, waits for them, and re-layouts  64.1 us (30%)
  starting transfers between devices  41.2 us (19%)
  matrix products  10.3 us (5%)
  blocking collectives  8.01 us (4%)
  other arithmetic  4.31 us (2%)
    all_to_all x1, waiting for transfers between devices, on_device(): lax.all_to_all(stacked.reshape(stack_rows, local_x, local_yz), 'gx', spli...  48.1 us
    unnamed x24, local copies, waits for them, and re-layouts  30.1 us
    all_to_all x1, starting transfers between devices, on_device(): lax.all_to_all(stacked.reshape(stack_rows, local_x, local_yz), 'gx', spli...  13.8 us
    all_to_all x1, local copies, waits for them, and re-layouts, on_device(): lax.all_to_all(stacked.reshape(stack_rows, local_x, local_yz), 'gx', spli...  9.24 us
    all_to_all x1, waiting for transfers between devices, on_device(): lax.all_to_all(back_y, 'gx', split_axis=2, concat_axis=1, tiled=True)  8.58 us
    all_to_all x1, waiting for transfers between devices, on_device(): lax.all_to_all(x_spectra, 'gx', split_axis=1, concat_axis=2, tiled=True)  8.52 us
    reshape x1, local copies, waits for them, and re-layouts, on_device(): stacked.reshape(stack_rows, local_x, local_yz)  8.04 us
    all_gather x1, blocking collectives, on_device(): all_gather(weight_grads(field_hat, grad_scaled).astype(jnp.bfloat16), axi...  8.01 us
  transfers between devices with their start and end apart: 6, of which 6 were waited for; matrix products, arithmetic and copies ran while one was open for 1% of the time, Pallas kernels for 0%

profile of v1, /device:TPU:1, one launch (start us, length us, event | category | flops | bytes accessed | tf_op | source)
XLA Modules:
  0.0 209.9 jit_solution(12966531480754730534)
XLA Ops:
  0.7 2.3 %fusion.11 = bf16[1,16,8,4096]{3,2,1,0:T(8,128)(2,1)S(1)} fusion(bf16[1,16,8,4096]{3,2,1,0:T(8,128)(2,1)} %param.6, bf16[1,16,8,4096]{3,2,1,0:T(8,128)(2,1)} %param.7), kind=kLoop, calls=%fused_computation.17 | loop fusion | flops 6291456 | bytes 3145728 | tf_op jit(solution)/shard_map/convert_element_type | solution.py:116
  3.2 8.0 %copy.202 = bf16[32,8,4096]{0,1,2:T(8,128)(2,1)} copy(bf16[32,8,4096]{2,1,0:T(8,128)(2,1)S(1)} %bitcast.229) | data formatting | bytes 4194304 | tf_op jit(solution)/shard_map/reshape | solution.py:122
  11.2 13.3 %reshape.1038 = bf16[32,2,16384]{2,1,0:T(2,128)(2,1)} reshape(bf16[4096,8,32]{2,1,0:T(8,128)(2,1)} %bitcast.226) | data formatting | bytes 4194304
  24.5 13.8 %all-to-all-start = ((bf16[32,2,16384]{2,1,0:T(2,128)(2,1)}), bf16[32,2,16384]{2,1,0:T(2,128)(2,1)S(1)}, u32[]{:S(2)}, u32[]{:S(2)}) async-start(bf16[32,2,16384]{2,1,0:T(2,128)(2,1)} %reshape.1038), calls=%async_computation | async-start | bytes 4194304 | tf_op jit(solution)/shard_map/all_to_all | solution.py:121
  39.2 48.1 %all-to-all-done = bf16[32,2,16384]{2,1,0:T(2,128)(2,1)S(1)} async-done(((bf16[32,2,16384]{2,1,0:T(2,128)(2,1)}), bf16[32,2,16384]{2,1,0:T(2,128)(2,1)S(1)}, u32[]{:S(2)}, u32[]{:S(2)}) %all-to-all-start) | async-done | bytes 2097184 | tf_op jit(solution)/shard_map/all_to_all | solution.py:121
  87.3 6.5 %reshape.1039 = bf16[4096,8,32]{2,1,0:T(8,128)(2,1)} reshape(bf16[32,2,16384]{2,1,0:T(2,128)(2,1)S(1)} %all-to-all-done) | data formatting | bytes 4194304
  93.8 9.2 %copy.204 = bf16[32,32,8,128]{3,2,1,0:T(8,128)(2,1)S(1)} copy(bf16[32,32,8,128]{0,2,3,1:T(8,128)(2,1)} %bitcast.227) | data formatting | bytes 4194304 | tf_op jit(solution)/shard_map/all_to_all | solution.py:121
  103.1 3.3 %reshape.994 = bf16[32,256,2,64]{3,2,1,0:T(2,128)(2,1)} reshape(bf16[32,32,8,128]{3,2,1,0:T(8,128)(2,1)S(1)} %copy.204) | data formatting | bytes 4194304 | tf_op jit(solution)/shard_map/reshape | solution.py:129
  106.4 3.7 %fusion.12 = bf16[32,256,2,32]{1,3,2,0:T(8,128)(2,1)S(1)} fusion(bf16[64,32,1,1]{0,1,3,2:T(8,128)(2,1)S(1)} %bitcast.250, bf16[32,256,2,64]{3,2,1,0:T(2,128)(2,1)} %reshape.994), kind=kOutput, calls=%fused_computation.18 | convolution fusion | flops 67633152 | bytes 3149824 | tf_op jit(solution)/shard_map/dot_general | solution.py:128
  113.9 7.0 %all-to-all-start.1 = ((bf16[32,2,1024]{2,1,0:T(2,128)(2,1)}), bf16[32,2,1024]{2,1,0:T(2,128)(2,1)S(1)}, u32[]{:S(2)}, u32[]{:S(2)}) async-start(bf16[32,2,1024]{2,1,0:T(2,128)(2,1)} %reshape.1040), calls=%async_computation.1 | async-start | bytes 262144 | tf_op jit(solution)/shard_map/all_to_all | solution.py:137
  121.6 8.5 %all-to-all-done.1 = bf16[32,2,1024]{2,1,0:T(2,128)(2,1)S(1)} async-done(((bf16[32,2,1024]{2,1,0:T(2,128)(2,1)}), bf16[32,2,1024]{2,1,0:T(2,128)(2,1)S(1)}, u32[]{:S(2)}, u32[]{:S(2)}) %all-to-all-start.1) | async-done | bytes 131104 | tf_op jit(solution)/shard_map/all_to_all | solution.py:137
  131.9 7.2 %all-to-all-start.2 = ((bf16[8,2,4096]{2,1,0:T(2,128)(2,1)}), bf16[8,2,4096]{2,1,0:T(2,128)(2,1)S(1)}, u32[]{:S(2)}, u32[]{:S(2)}) async-start(bf16[8,2,4096]{2,1,0:T(2,128)(2,1)} %reshape.1042), calls=%async_computation.2 | async-start | bytes 262144 | tf_op jit(solution)/shard_map/all_to_all | solution.py:136
  139.1 5.7 %all-to-all-done.2 = bf16[8,2,4096]{2,1,0:T(2,128)(2,1)S(1)} async-done(((bf16[8,2,4096]{2,1,0:T(2,128)(2,1)}), bf16[8,2,4096]{2,1,0:T(2,128)(2,1)S(1)}, u32[]{:S(2)}, u32[]{:S(2)}) %all-to-all-start.2) | async-done | bytes 131104 | tf_op jit(solution)/shard_map/all_to_all | solution.py:136
  147.9 3.9 %all-to-all-start.3 = ((bf16[32,2,512]{2,1,0:T(2,128)(2,1)}), bf16[32,2,512]{2,1,0:T(2,128)(2,1)S(1)}, u32[]{:S(2)}, u32[]{:S(2)}) async-start(bf16[32,2,512]{2,1,0:T(2,128)(2,1)} %reshape.1044), calls=%async_computation.3 | async-start | bytes 131072 | tf_op jit(solution)/shard_map/all_to_all | solution.py:170
  152.0 8.6 %all-to-all-done.3 = bf16[32,2,512]{2,1,0:T(2,128)(2,1)S(1)} async-done(((bf16[32,2,512]{2,1,0:T(2,128)(2,1)}), bf16[32,2,512]{2,1,0:T(2,128)(2,1)S(1)}, u32[]{:S(2)}, u32[]{:S(2)}) %all-to-all-start.3) | async-done | bytes 65568 | tf_op jit(solution)/shard_map/all_to_all | solution.py:170
  162.5 5.4 %all-to-all-start.4 = ((bf16[8,2,2048]{2,1,0:T(2,128)(2,1)}), bf16[8,2,2048]{2,1,0:T(2,128)(2,1)S(1)}, u32[]{:S(2)}, u32[]{:S(2)}) async-start(bf16[8,2,2048]{2,1,0:T(2,128)(2,1)} %reshape.1046), calls=%async_computation.4 | async-start | bytes 131072 | tf_op jit(solution)/shard_map/all_to_all | solution.py:169
  167.9 5.0 %all-to-all-done.4 = bf16[8,2,2048]{2,1,0:T(2,128)(2,1)S(1)} async-done(((bf16[8,2,2048]{2,1,0:T(2,128)(2,1)}), bf16[8,2,2048]{2,1,0:T(2,128)(2,1)S(1)}, u32[]{:S(2)}, u32[]{:S(2)}) %all-to-all-start.4) | async-done | bytes 65568 | tf_op jit(solution)/shard_map/all_to_all | solution.py:169
  176.7 3.9 %all-to-all-start.5 = ((bf16[32,2,4096]{2,1,0:T(2,128)(2,1)}), bf16[32,2,4096]{2,1,0:T(2,128)(2,1)S(1)}, u32[]{:S(2)}, u32[]{:S(2)}) async-start(bf16[32,2,4096]{2,1,0:T(2,128)(2,1)} %reshape.1048), calls=%async_computation.5 | async-start | bytes 1048576 | tf_op jit(solution)/shard_map/all_to_all | solution.py:183
  180.9 8.0 %all_gather.4 = bf16[2,2,1,32,2,256]{5,3,4,2,1,0:T(8,128)(2,1)S(1)} all-gather(bf16[1,2,1,32,2,256]{5,3,4,2,1,0:T(8,128)(2,1)S(1)} %pad_maximum_fusion.1), channel_id=1, replica_groups=mesh['dp'=2,'gx'=32,'gy'=8] {'dp'}, dimensions={0}, use_global_device_ids=true | all-gather | bytes 196608 | tf_op jit(solution)/shard_map/all_gather | solution.py:154
  190.0 4.9 %all-to-all-done.5 = bf16[32,2,4096]{2,1,0:T(2,128)(2,1)S(1)} async-done(((bf16[32,2,4096]{2,1,0:T(2,128)(2,1)}), bf16[32,2,4096]{2,1,0:T(2,128)(2,1)S(1)}, u32[]{:S(2)}, u32[]{:S(2)}) %all-to-all-start.5) | async-done | bytes 524320 | tf_op jit(solution)/shard_map/all_to_all | solution.py:183
  197.1 2.7 %reshape.1005 = bf16[16,8,64,32]{3,2,1,0:T(8,128)(2,1)S(1)} reshape(bf16[16,8,32,64]{3,2,1,0:T(8,128)(2,1)} %copy.224) | data formatting | bytes 1048576 | tf_op jit(solution)/shard_map/reshape | solution.py:187
  199.9 2.6 %fusion.103 = f32[16,8,64,64]{3,2,1,0:T(8,128)} fusion(bf16[16,8,64,32]{3,2,1,0:T(8,128)(2,1)S(1)} %reshape.1005, bf16[32,64,1,1]{1,0,3,2:T(8,128)(2,1)S(1)} %bitcast.249), kind=kOutput, calls=%fused_computation.191 | convolution fusion | flops 33554432 | bytes 2625536 | tf_op jit(solution)/shard_map/dot_general | solution.py:186
  202.5 3.5 %reshape.1006 = f32[1,16,8,4096]{3,2,1,0:T(8,128)S(1)} reshape(f32[16,8,64,64]{3,2,1,0:T(8,128)} %fusion.103) | data formatting | bytes 4194304 | tf_op jit(solution)/shard_map/reshape | solution.py:191
  206.1 2.3 %fusion.1 = bf16[1,16,8,4096]{3,1,2,0:T(8,128)(2,1)S(1)} fusion(f32[1,16,8,4096]{3,2,1,0:T(8,128)S(1)} %reshape.1006, bf16[16,8,4096]{2,1,0:T(8,128)(2,1)S(1)} %bitcast.228, bf16[16,16]{1,0:T(8,128)(2,1)S(1)} %copy-done), kind=kOutput, calls=%fused_computation.2 | convolution fusion | flops 17825792 | bytes 4194816 | tf_op jit(solution)/shard_map/io,boxq->bixq/dot_general | solution.py:192
  (71 shorter events, 21.2 us)
Async XLA Ops:
  0.6 205.4 %copy-start = (bf16[16,16]{1,0:T(8,128)(2,1)S(1)}, bf16[16,16]{1,0:T(8,128)(2,1)}, u32[]{:S(2)}) copy-start(bf16[16,16]{1,0:T(8,128)(2,1)} %param.9) | copy-start | bytes 1540
  0.6 2.3 %copy-start.1 = (bf16[1,16,8,4096]{3,2,1,0:T(8,128)(2,1)S(1)}, bf16[1,16,8,4096]{3,2,1,0:T(8,128)(2,1)}, u32[]{:S(2)}) copy-start(bf16[1,16,8,4096]{3,2,1,0:T(8,128)(2,1)} %param.5) | copy-start | bytes 3145732
  24.5 14.2 %copy-start.2 = (bf16[2,1,32,2,256]{4,3,2,1,0:T(2,128)(2,1)S(1)}, bf16[2,1,32,2,256]{4,3,2,1,0:T(2,128)(2,1)}, u32[]{:S(2)}) copy-start(bf16[2,1,32,2,256]{4,3,2,1,0:T(2,128)(2,1)} %param.8) | copy-start | bytes 196612
  24.5 62.7 %all-to-all-start = ((bf16[32,2,16384]{2,1,0:T(2,128)(2,1)}), bf16[32,2,16384]{2,1,0:T(2,128)(2,1)S(1)}, u32[]{:S(2)}, u32[]{:S(2)}) async-start(bf16[32,2,16384]{2,1,0:T(2,128)(2,1)} %reshape.1038), calls=%async_computation | async-start | bytes 4194304 | tf_op jit(solution)/shard_map/all_to_all | solution.py:121
  113.9 16.2 %all-to-all-start.1 = ((bf16[32,2,1024]{2,1,0:T(2,128)(2,1)}), bf16[32,2,1024]{2,1,0:T(2,128)(2,1)S(1)}, u32[]{:S(2)}, u32[]{:S(2)}) async-start(bf16[32,2,1024]{2,1,0:T(2,128)(2,1)} %reshape.1040), calls=%async_computation.1 | async-start | bytes 262144 | tf_op jit(solution)/shard_map/all_to_all | solution.py:137
  131.9 13.0 %all-to-all-start.2 = ((bf16[8,2,4096]{2,1,0:T(2,128)(2,1)}), bf16[8,2,4096]{2,1,0:T(2,128)(2,1)S(1)}, u32[]{:S(2)}, u32[]{:S(2)}) async-start(bf16[8,2,4096]{2,1,0:T(2,128)(2,1)} %reshape.1042), calls=%async_computation.2 | async-start | bytes 262144 | tf_op jit(solution)/shard_map/all_to_all | solution.py:136
  147.9 12.7 %all-to-all-start.3 = ((bf16[32,2,512]{2,1,0:T(2,128)(2,1)}), bf16[32,2,512]{2,1,0:T(2,128)(2,1)S(1)}, u32[]{:S(2)}, u32[]{:S(2)}) async-start(bf16[32,2,512]{2,1,0:T(2,128)(2,1)} %reshape.1044), calls=%async_computation.3 | async-start | bytes 131072 | tf_op jit(solution)/shard_map/all_to_all | solution.py:170
  162.5 10.5 %all-to-all-start.4 = ((bf16[8,2,2048]{2,1,0:T(2,128)(2,1)}), bf16[8,2,2048]{2,1,0:T(2,128)(2,1)S(1)}, u32[]{:S(2)}, u32[]{:S(2)}) async-start(bf16[8,2,2048]{2,1,0:T(2,128)(2,1)} %reshape.1046), calls=%async_computation.4 | async-start | bytes 131072 | tf_op jit(solution)/shard_map/all_to_all | solution.py:169
  176.7 18.2 %all-to-all-start.5 = ((bf16[32,2,4096]{2,1,0:T(2,128)(2,1)}), bf16[32,2,4096]{2,1,0:T(2,128)(2,1)S(1)}, u32[]{:S(2)}, u32[]{:S(2)}) async-start(bf16[32,2,4096]{2,1,0:T(2,128)(2,1)} %reshape.1048), calls=%async_computation.5 | async-start | bytes 1048576 | tf_op jit(solution)/shard_map/all_to_all | solution.py:183
